TPU v7x, 32 devices: a whole 2x2x4 slice. The times are simulated.
32 devices in a mesh: dp: 8 (over y, x, core), mp: 4 (over z).
Axes of the slice: x: 2, y: 2, z: 4, core: 2. Of those that a mesh axis runs over, the one named last changes fastest.
Arguments:
- gen_rows: bfloat16 [1024, 5120], P(('dp', 'mp')), may hold values from -6 to 6
- lengths: int32 [32, 4], P('dp'), may hold values from 1 to 16, 32 in all within a row
- assign: int32 [32, 4], P('dp'), may hold values from 0 to 3, each once within a row
- rewards: float32 [32, 4], P('dp'), may hold values from 0 to 1
- upstream: bfloat16 [2048, 2048], P('dp', 'mp'), may hold values from -6 to 6
- weight: bfloat16 [5120, 2048], P(None, 'mp'), may hold values from -0.078125 to 0.078125
- q_init: float32 [2048, 64], P('mp'), may hold values from -6 to 6
- resid: float32 [32, 128, 2048], P('dp', None, 'mp'), may hold values from -4 to 4
- block_ids: int32 [32], P('dp'), may hold values from 0 to 39, as said below
Outputs:
- p_factor: float32 [5120, 256], P(None, 'mp')
- q_factor: float32 [2048, 64], P('mp')
- resid_out: float32 [32, 128, 2048], P('dp', None, 'mp')
Inputs may be any that keep to these rules, and one draw needn't show every extreme that they name: Each row holds the lengths of one generator's 4 sequences; they sum to 32. `assign`: each row names every learner once. `block_ids`: the 4 ids of one replica are distinct.
All inputs are finite; a program needn't handle non-finite values.
Results may differ from a plain program's by a relative error of at most 0.003.
Values may be sent and summed in bfloat16 or wider, within the bound.
No kernel may reach another device: no remote copies, remote signals or barrier semaphores. Data moves between devices by JAX's collectives and lax.ppermute only.
A program may use at most 64 MiB of HBM per device.

v0:
```python
import jax
import jax.numpy as jnp
from jax import lax
from jax.sharding import PartitionSpec as P

HIGHEST_PRECISION = lax.Precision.HIGHEST


def packed_tables(lengths, assign, rewards, slot_count, capacity):
    groups, sequences = lengths.shape
    offsets = jnp.cumsum(lengths, axis=1) - lengths
    advantage = rewards - jnp.mean(rewards, axis=1, keepdims=True)
    seq_weight = advantage / lengths.astype(rewards.dtype)
    positions = jnp.arange(slot_count)
    seq_index = jnp.arange(sequences)
    inside = (offsets[:, None, :] <= positions[None, :, None]).astype(jnp.int32)
    owner = jnp.sum(inside, axis=2) - 1
    picked = owner[:, :, None] == seq_index[None, None, :]
    seq_start = jnp.sum(jnp.where(picked, offsets[:, None, :], 0), axis=2)
    learner = jnp.sum(jnp.where(picked, assign[:, None, :], 0), axis=2)
    row_weight = jnp.sum(jnp.where(picked, seq_weight[:, None, :], 0.0), axis=2)
    source = jnp.arange(groups)[:, None]
    slot_table = learner * (groups * capacity) + source * capacity + positions[None, :] - seq_start
    return (slot_table, row_weight)


def row_gradient(row_block, upstream_rows, weights_here, weight):
    hidden = jnp.dot(row_block, weight, preferred_element_type=jnp.float32)
    tangent = jnp.tanh(hidden)
    grad_h = (
        weights_here[:, None] * upstream_rows.astype(jnp.float32) * (1.0 - tangent * tangent)
    ).astype(jnp.bfloat16)
    return jnp.einsum("nd,nc->dc", row_block, grad_h, preferred_element_type=jnp.float32)


def shards(gen_rows, lengths, assign, rewards, upstream, weight, q_init, resid, block_ids):
    groups = lax.axis_size("mp")
    slot_count = gen_rows.shape[0]
    capacity = upstream.shape[0] // (groups * groups)
    slot_table, row_weight = packed_tables(lengths, assign, rewards, slot_count, capacity)
    flat_slot = slot_table.reshape(-1)
    flat_weight = row_weight.reshape(-1)
    upstream_rows = jnp.take(upstream, flat_slot, axis=0)
    gradient = row_gradient(
        lax.all_gather(gen_rows, "mp", axis=0, tiled=True), upstream_rows, flat_weight, weight
    )
    block_rows = resid.shape[1]
    for block in range(resid.shape[0]):
        first_row = block_ids[block] * block_rows
        current = lax.dynamic_slice_in_dim(gradient, first_row, block_rows, 0)
        gradient = lax.dynamic_update_slice_in_dim(gradient, current + resid[block], first_row, 0)
    p_local = jnp.dot(gradient, q_init, precision=HIGHEST_PRECISION)
    p_sum = lax.psum(p_local, "dp")
    gram_matrix = jnp.einsum("dr,ds->rs", p_sum, p_sum, precision=HIGHEST_PRECISION)
    factor_low = jnp.linalg.cholesky(gram_matrix)
    p_factor = jax.scipy.linalg.solve_triangular(factor_low, p_sum.T, lower=True).T
    q_local = jnp.einsum("dc,dr->cr", gradient, p_factor, precision=HIGHEST_PRECISION)
    q_factor = lax.psum(q_local, "dp") / lax.axis_size("dp")
    new_blocks = []
    for block in range(resid.shape[0]):
        first_row = block_ids[block] * block_rows
        merged_rows = lax.dynamic_slice_in_dim(gradient, first_row, block_rows, 0)
        p_rows = lax.dynamic_slice_in_dim(p_factor, first_row, block_rows, 0)
        approx = jnp.einsum("br,cr->bc", p_rows, q_factor, precision=HIGHEST_PRECISION)
        new_blocks.append(merged_rows - approx)
    return (p_factor, q_factor, jnp.stack(new_blocks))


def solution(mesh):
    placed = (
        P(("dp", "mp"), None),
        P("dp", None),
        P("dp", None),
        P("dp", None),
        P("dp", "mp"),
        P(None, "mp"),
        P("mp", None),
        P("dp", None, "mp"),
        P("dp"),
    )
    return jax.shard_map(
        shards,
        mesh=mesh,
        in_specs=placed,
        out_specs=(P(None, "mp"), P("mp", None), P("dp", None, "mp")),
        check_vma=False,
    )
```

profile of v0, /device:TPU:0, one launch (start us, length us, event | category | flops | bytes accessed | tf_op | source)
XLA Modules:
  0.0 227.9 jit_solution(15444329244682934595)
XLA Ops:
  7.2 0.0 copy-start
  7.2 0.0 all-gather.2.cloned.1.call-start
  7.2 0.7 all-gather.2.cloned.1.call-update
  7.9 0.0 all-reduce.3.cloned.1.call-start
  8.0 0.9 reduce_window_sum.11
  8.8 0.7 sub.52
  9.5 0.1 convert_reduce_fusion
  9.6 0.8 select_reduce_fusion.2
  10.4 0.1 add_subtract_fusion
  10.5 0.1 sub.58
  10.5 0.1 sub.57
  10.6 1.5 fusion.36
  14.8 0.8 reduce_sum.46
  15.6 0.8 convert_divide_fusion
  16.3 0.1 select_reduce_fusion.3
  16.4 0.1 mul.70
  16.5 1.3 fusion.35
  17.8 0.1 copy.39
  17.9 0.1 copy.38
  18.0 0.1 copy.37
  18.2 0.1 copy.36
  18.3 0.0 copy-done
  18.4 0.8 gather_fusion
  19.2 25.8 %all-gather.2.cloned.1.call-done = bf16[128,5120]{1,0:T(8,128)(2,1)} async-done(((bf16[32,5120]{1,0:T(8,128)(2,1)}), bf16[128,5120]{1,0:T(8,128)(2,1)}) %all-gather.2.cloned.1.call-update) | async-done | bytes 1310736 | tf_op jit(solution)/shard_map/all_gather | solution.py:45
  45.0 9.6 %fusion.8 = f32[512,5120]{1,0:T(8,128)} fusion(bf16[128,5120]{1,0:T(8,128)(2,1)} %all-gather.2.cloned.1.call-done, bf16[5120,512]{1,0:T(8,128)(2,1)} %param.14, bf16[128,512]{1,0:T(8,128)(2,1)S(1)} %gather_fusion, f32[128]{0:T(128)S(1)} %mul.70, pred[128]{0:T(512)(128)(4,1)S(1)} %compare_and_fusion), kind=kOutput, calls=%fused_computation.14 | convolution fusion | flops 1342636032 | bytes 17171072 | tf_op jit(solution)/shard_map/nd,nc->dc/dot_general | solution.py:33
  54.6 0.0 copy-start.4
  54.6 4.0 %copy.40 = f32[5120,512]{0,1:T(8,128)S(1)} copy(f32[5120,512]{0,1:T(8,128)} %bitcast.57) | data formatting | bytes 20971520
  58.7 1.0 fusion.12
  59.6 0.1 fusion.11
  59.7 0.1 fusion.10
  59.8 0.1 fusion.9
  59.9 0.0 copy-start.1
  59.9 4.0 %copy-done.1 = f32[5120,512]{0,1:T(8,128)} copy-done((f32[5120,512]{0,1:T(8,128)}, f32[5120,512]{0,1:T(8,128)S(1)}, u32[]{:S(2)}) %copy-start.1) | copy-done | bytes 10485784
  63.9 0.0 copy-done.4
  63.9 8.0 %fusion.37 = f32[5120,64]{0,1:T(8,128)} fusion(f32[5120,512]{0,1:T(8,128)S(1)} %fusion.9, f32[512,64]{0,1:T(8,128)S(1)} %copy-done.4), kind=kOutput, calls=%fused_computation.70 | convolution fusion | flops 2013265920 | bytes 11927552 | tf_op jit(solution)/shard_map/dot_general | solution.py:52
  71.9 0.0 all-reduce.3.cloned.1.call-update
  72.0 0.2 all-reduce.5.cloned.1.call-start
  72.2 56.7 %all-reduce.3.cloned.1.call-done = f32[5120,64]{0,1:T(8,128)} async-done(((f32[5120,64]{0,1:T(8,128)}), f32[5120,64]{0,1:T(8,128)}) %all-reduce.3.cloned.1.call-update) | async-done | bytes 1310736 | tf_op jit(solution)/shard_map/psum | solution.py:53
  128.9 2.9 %fusion.38 = f32[64,64]{1,0:T(8,128)S(1)} fusion(f32[5120,64]{0,1:T(8,128)} %all-reduce.3.cloned.1.call-done), kind=kOutput, calls=%fused_computation.71 | convolution fusion | flops 251658240 | bytes 1327104 | tf_op jit(solution)/shard_map/dr,ds->rs/dot_general | solution.py:54
  131.8 0.1 copy.26
  131.9 5.8 %cholesky.16 = f32[64,64]{1,0:T(8,128)S(1)} custom-call(f32[64,64]{1,0:T(8,128)S(1)} %fusion.23), custom_call_target="Cholesky" | custom-call | tf_op jit(solution)/shard_map/jit(cholesky)/cholesky | solution.py:55
  137.7 0.6 compare_reduce_fusion
  138.4 0.7 fusion.20
  139.0 4.9 %custom-call.7 = f32[1,64,64]{1,2,0:T(8,128)S(1)} custom-call(f32[1,64,64]{2,1,0:T(8,128)S(1)} %fusion.20), custom_call_target="InvertDiagBlocksLowerTriangular" | custom-call | tf_op jit(solution)/shard_map/jit(_solve_triangular)/triangular_solve | solution.py:56
  143.9 2.6 %fusion.21 = f32[64,5120]{1,0:T(8,128)S(1)} fusion(f32[5120,64]{0,1:T(8,128)} %all-reduce.3.cloned.1.call-done, f32[1,64,64]{1,2,0:T(8,128)S(1)} %custom-call.7), kind=kOutput, calls=%fused_computation.34 | convolution fusion | flops 251658240 | bytes 2637824 | tf_op jit(solution)/shard_map/jit(_solve_triangular)/triangular_solve | solution.py:56
  146.5 0.0 copy-start.2
  146.5 13.9 %fusion.39 = f32[512,64]{0,1:T(8,128)} fusion(f32[5120,512]{0,1:T(8,128)} %copy-done.1, f32[64,5120]{1,0:T(8,128)S(1)} %fusion.21), kind=kOutput, calls=%fused_computation.72 | convolution fusion | flops 2013265920 | bytes 11927552 | tf_op jit(solution)/shard_map/dc,dr->cr/dot_general | solution.py:57
  160.4 0.0 all-reduce.5.cloned.1.call-update
  160.5 52.3 %all-reduce.5.cloned.1.call-done = f32[512,64]{0,1:T(8,128)} async-done(((f32[512,64]{0,1:T(8,128)}), f32[512,64]{0,1:T(8,128)}) %all-reduce.5.cloned.1.call-update) | async-done | bytes 131088 | tf_op jit(solution)/shard_map/psum | solution.py:58
  212.7 0.9 broadcast_multiply_fusion
  213.7 0.0 copy-start.3
  213.7 1.6 fusion
  215.3 1.6 fusion.1
  216.8 1.6 fusion.2
  218.4 0.0 copy-done.2
  218.4 1.6 fusion.3
  220.0 0.1 pad_maximum_fusion
  220.1 1.3 copy.31
  221.4 0.0 copy-done.3
  (8 shorter events, 0.1 us)
Async XLA Ops:
  7.2 11.2 %copy-start = (bf16[256,512]{1,0:T(8,128)(2,1)S(1)}, bf16[256,512]{1,0:T(8,128)(2,1)}, u32[]{:S(2)}) copy-start(bf16[256,512]{1,0:T(8,128)(2,1)} %param.13) | copy-start | bytes 786436
  7.2 37.8 %all-gather.2.cloned.1.call-start = ((), (), s32[]{:S(2)}) async-start(), calls=%async_computation | async-start | bytes 1638400 | tf_op jit(solution)/shard_map/all_gather | solution.py:45
  7.9 120.9 %all-reduce.3.cloned.1.call-start = ((), (), s32[]{:S(2)}) async-start(), calls=%async_computation.1 | async-start | bytes 2621440 | tf_op jit(solution)/shard_map/psum | solution.py:53
  54.6 9.2 %copy-start.4 = (f32[512,64]{0,1:T(8,128)S(1)}, f32[512,64]{0,1:T(8,128)}, u32[]{:S(2)}) copy-start(f32[512,64]{0,1:T(8,128)} %param.15) | copy-start | bytes 393220
  59.9 4.0 %copy-start.1 = (f32[5120,512]{0,1:T(8,128)}, f32[5120,512]{0,1:T(8,128)S(1)}, u32[]{:S(2)}) copy-start(f32[5120,512]{0,1:T(8,128)S(1)} %fusion.9) | copy-start | bytes 31457284
  72.0 140.8 %all-reduce.5.cloned.1.call-start = ((), (), s32[]{:S(2)}) async-start(), calls=%async_computation.2 | async-start | bytes 262144 | tf_op jit(solution)/shard_map/psum | solution.py:58
  146.5 71.9 %copy-start.2 = (f32[64,5120]{1,0:T(8,128)}, f32[64,5120]{1,0:T(8,128)S(1)}, u32[]{:S(2)}) copy-start(f32[64,5120]{1,0:T(8,128)S(1)} %fusion.21) | copy-start | bytes 3932164
  213.7 7.7 %copy-start.3 = (f32[512,64]{0,1:T(8,128)}, f32[512,64]{0,1:T(8,128)S(1)}, u32[]{:S(2)}) copy-start(f32[512,64]{0,1:T(8,128)S(1)} %broadcast_multiply_fusion) | copy-start | bytes 393220
Sparse Core Ops, SparseCore 0:
  9.6 35.3 all-gather.1
  72.1 56.7 all-reduce.2
  160.6 52.1 all-reduce.4
where the time goes:
time: 228 us
  waiting for transfers between devices  135 us (59%)
  matrix products  43.3 us (19%)
  other arithmetic  18.4 us (8%)
  between operations  16.7 us (7%)
  local copies, waits for them, and re-layouts  13.7 us (6%)
    psum x1, waiting for transfers between devices, shards(): p_sum = lax.psum(p_local, 'dp')  56.7 us
    psum x1, waiting for transfers between devices, shards(): q_factor = lax.psum(q_local, 'dp') / lax.axis_size('dp')  52.3 us
    all_gather x1, waiting for transfers between devices, shards(): lax.all_gather(gen_rows, 'mp', axis=0, tiled=True)  25.8 us
    dot_general x1, matrix products, shards(): jnp.einsum('dc,dr->cr', gradient, p_factor, precision=HIGHEST_PRECISION)  13.9 us
    unnamed x16, local copies, waits for them, and re-layouts  9.83 us
    dot_general x1, matrix products, row_gradient(): jnp.einsum('nd,nc->dc', row_block, grad_h, preferred_element_type=jnp.flo...  9.64 us
    dot_general x1, matrix products, shards(): p_local = jnp.dot(gradient, q_init, precision=HIGHEST_PRECISION)  8.05 us
    another operation x3, other arithmetic, shards(): factor_low = jnp.linalg.cholesky(gram_matrix)  6.52 us
  transfers between devices with their start and end apart: 3, of which 3 were waited for; matrix products, arithmetic and copies ran while one was open for 4% of the time, Pallas kernels for 0%

commit v1 on v0

--- a/solution.py
+++ b/solution.py
@@ -50,7 +50,7 @@
         current = lax.dynamic_slice_in_dim(gradient, first_row, block_rows, 0)
         gradient = lax.dynamic_update_slice_in_dim(gradient, current + resid[block], first_row, 0)
     p_local = jnp.dot(gradient, q_init, precision=HIGHEST_PRECISION)
-    p_sum = lax.psum(p_local, "dp")
+    p_sum = jnp.sum(lax.all_gather(p_local, "dp"), axis=0)
     gram_matrix = jnp.einsum("dr,ds->rs", p_sum, p_sum, precision=HIGHEST_PRECISION)
     factor_low = jnp.linalg.cholesky(gram_matrix)
     p_factor = jax.scipy.linalg.solve_triangular(factor_low, p_sum.T, lower=True).T

time: 228 us -> 245 us (1.075)
  local copies, waits for them, and re-layouts: 13.7 us -> 24 us
  waiting for transfers between devices: 135 us -> 142 us
  matrix products: 43.3 us -> 40.8 us
  other arithmetic: 18.4 us -> 20.9 us
    all_gather x0 -> x1, waiting for transfers between devices: none -> 62.2 us  [shards(): p_sum = jnp.sum(lax.all_gather(p_local, 'dp'), axis=0)]
    psum x1 -> x0, waiting for transfers between devices: 56.7 us -> none  [shards(): p_sum = lax.psum(p_local, 'dp')]
    unnamed x16 -> x15, local copies, waits for them, and re-layouts: 9.83 us -> 20 us
    reduce_sum x0 -> x1, other arithmetic: none -> 2.46 us  [shards(): p_sum = jnp.sum(lax.all_gather(p_local, 'dp'), axis=0)]
  transfers between devices with their start and end apart: 3 -> 3, of which waited for: 3 -> 3; matrix products, arithmetic and copies ran while one was open for 4% -> 3% of each run, Pallas kernels for 0% -> 0%
where the time goes in v1:
time: 245 us; the launch traced here: 244 us
  waiting for transfers between devices  142 us (58%)
  matrix products  40.8 us (17%)
  local copies, waits for them, and re-layouts  24 us (10%)
  other arithmetic  20.9 us (9%)
  between operations  16.6 us (7%)
    all_gather x1, waiting for transfers between devices, shards(): p_sum = jnp.sum(lax.all_gather(p_local, 'dp'), axis=0)  62.2 us
    psum x1, waiting for transfers between devices, shards(): q_factor = lax.psum(q_local, 'dp') / lax.axis_size('dp')  53.1 us
    all_gather x1, waiting for transfers between devices, shards(): lax.all_gather(gen_rows, 'mp', axis=0, tiled=True)  25.8 us
    unnamed x15, local copies, waits for them, and re-layouts  20 us
    dot_general x1, matrix products, shards(): jnp.einsum('dc,dr->cr', gradient, p_factor, precision=HIGHEST_PRECISION)  13 us
    dot_general x1, matrix products, row_gradient(): jnp.einsum('nd,nc->dc', row_block, grad_h, preferred_element_type=jnp.flo...  9.64 us
    dot_general x1, matrix products, shards(): p_local = jnp.dot(gradient, q_init, precision=HIGHEST_PRECISION)  8.05 us
    another operation x3, other arithmetic, shards(): factor_low = jnp.linalg.cholesky(gram_matrix)  6.52 us
  transfers between devices with their start and end apart: 3, of which 3 were waited for; matrix products, arithmetic and copies ran while one was open for 3% of the time, Pallas kernels for 0%

profile of v1, /device:TPU:0, one launch (start us, length us, event | category | flops | bytes accessed | tf_op | source)
XLA Modules:
  0.0 244.4 jit_solution(15489164073835107508)
XLA Ops:
  7.2 0.0 copy-start
  7.2 0.0 all-gather.4.cloned.1.call-start
  7.2 0.7 all-gather.4.cloned.1.call-update
  7.9 0.0 all-gather.6.cloned.1.call-start
  8.0 0.9 reduce_window_sum.11
  8.8 0.7 sub.52
  9.5 0.1 convert_reduce_fusion
  9.6 0.8 select_reduce_fusion.2
  10.4 0.1 add_subtract_fusion
  10.5 0.1 sub.58
  10.5 0.1 sub.57
  10.6 1.5 fusion.36
  14.8 0.8 reduce_sum.55
  15.6 0.8 convert_divide_fusion
  16.3 0.1 select_reduce_fusion.3
  16.4 0.1 mul.70
  16.5 1.3 fusion.35
  17.8 0.1 copy.49
  17.9 0.1 copy.48
  18.0 0.1 copy.47
  18.2 0.1 copy.46
  18.3 0.0 copy-done
  18.4 0.8 gather_fusion
  19.2 25.8 %all-gather.4.cloned.1.call-done = bf16[128,5120]{1,0:T(8,128)(2,1)} async-done(((bf16[32,5120]{1,0:T(8,128)(2,1)}), bf16[128,5120]{1,0:T(8,128)(2,1)}) %all-gather.4.cloned.1.call-update) | async-done | bytes 1310736 | tf_op jit(solution)/shard_map/all_gather | solution.py:45
  45.0 9.6 %fusion.8 = f32[512,5120]{1,0:T(8,128)} fusion(bf16[128,5120]{1,0:T(8,128)(2,1)} %all-gather.4.cloned.1.call-done, bf16[5120,512]{1,0:T(8,128)(2,1)} %param.14, bf16[128,512]{1,0:T(8,128)(2,1)S(1)} %gather_fusion, f32[128]{0:T(128)S(1)} %mul.70, pred[128]{0:T(512)(128)(4,1)S(1)} %compare_and_fusion), kind=kOutput, calls=%fused_computation.15 | convolution fusion | flops 1342636032 | bytes 17171072 | tf_op jit(solution)/shard_map/nd,nc->dc/dot_general | solution.py:33
  54.6 0.0 copy-start.3
  54.6 4.0 %copy.51 = f32[5120,512]{0,1:T(8,128)S(1)} copy(f32[5120,512]{0,1:T(8,128)} %bitcast.62) | data formatting | bytes 20971520
  58.7 1.0 fusion.12
  59.6 0.1 fusion.11
  59.7 0.1 fusion.10
  59.8 0.1 fusion.9
  59.9 0.0 copy-start.1
  59.9 4.0 %copy-done.1 = f32[5120,512]{0,1:T(8,128)} copy-done((f32[5120,512]{0,1:T(8,128)}, f32[5120,512]{0,1:T(8,128)S(1)}, u32[]{:S(2)}) %copy-start.1) | copy-done | bytes 10485784
  63.9 0.0 copy-done.3
  63.9 8.0 %fusion.37 = f32[5120,64]{0,1:T(8,128)} fusion(f32[5120,512]{0,1:T(8,128)S(1)} %fusion.9, f32[512,64]{0,1:T(8,128)S(1)} %copy-done.3), kind=kOutput, calls=%fused_computation.71 | convolution fusion | flops 2013265920 | bytes 11927552 | tf_op jit(solution)/shard_map/dot_general | solution.py:52
  71.9 0.0 all-gather.6.cloned.1.call-update
  72.0 0.2 all-reduce.2.cloned.1.call-start
  72.2 62.2 %all-gather.6.cloned.1.call-done = f32[40960,64]{0,1:T(8,128)} async-done(((f32[5120,64]{0,1:T(8,128)}), f32[40960,64]{0,1:T(8,128)}) %all-gather.6.cloned.1.call-update) | async-done | bytes 10485776 | tf_op jit(solution)/shard_map/all_gather | solution.py:53
  134.4 10.2 %copy.50 = f32[8,8,8,5120]{3,2,1,0:T(8,128)S(1)} copy(f32[8,8,8,5120]{3,1,2,0:T(8,128)} %bitcast.63) | data formatting | bytes 20971520
  144.6 2.5 %bitcast_reduce_fusion = f32[5120,64]{0,1:T(8,128)S(1)} fusion(f32[8,8,8,5120]{3,2,1,0:T(8,128)S(1)} %copy.50), kind=kLoop, calls=%fused_computation.1 | loop fusion | flops 2293760 | bytes 11796480 | tf_op jit(solution)/shard_map/reduce_sum | solution.py:53
  147.1 1.2 fusion.38
  148.2 0.1 copy.36
  148.3 5.8 %cholesky.16 = f32[64,64]{1,0:T(8,128)S(1)} custom-call(f32[64,64]{1,0:T(8,128)S(1)} %fusion.23), custom_call_target="Cholesky" | custom-call | tf_op jit(solution)/shard_map/jit(cholesky)/cholesky | solution.py:55
  154.2 0.6 compare_reduce_fusion
  154.9 0.7 fusion.20
  155.5 4.9 %custom-call.7 = f32[1,64,64]{1,2,0:T(8,128)S(1)} custom-call(f32[1,64,64]{2,1,0:T(8,128)S(1)} %fusion.20), custom_call_target="InvertDiagBlocksLowerTriangular" | custom-call | tf_op jit(solution)/shard_map/jit(_solve_triangular)/triangular_solve | solution.py:56
  160.4 2.6 %fusion.21 = f32[64,5120]{1,0:T(8,128)} fusion(f32[5120,64]{0,1:T(8,128)S(1)} %bitcast_reduce_fusion, f32[1,64,64]{1,2,0:T(8,128)S(1)} %custom-call.7), kind=kOutput, calls=%fused_computation.35 | convolution fusion | flops 251658240 | bytes 2637824 | tf_op jit(solution)/shard_map/jit(_solve_triangular)/triangular_solve | solution.py:56
  163.0 13.0 %fusion.39 = f32[512,64]{0,1:T(8,128)} fusion(f32[5120,512]{0,1:T(8,128)} %copy-done.1, f32[64,5120]{1,0:T(8,128)} %fusion.21), kind=kOutput, calls=%fused_computation.73 | convolution fusion | flops 2013265920 | bytes 11927552 | tf_op jit(solution)/shard_map/dc,dr->cr/dot_general | solution.py:57
  176.0 0.0 all-reduce.2.cloned.1.call-update
  176.0 53.1 %all-reduce.2.cloned.1.call-done = f32[512,64]{0,1:T(8,128)} async-done(((f32[512,64]{0,1:T(8,128)}), f32[512,64]{0,1:T(8,128)}) %all-reduce.2.cloned.1.call-update) | async-done | bytes 131088 | tf_op jit(solution)/shard_map/psum | solution.py:58
  229.2 0.9 broadcast_multiply_fusion
  230.1 0.0 copy-start.2
  230.1 1.6 fusion
  231.7 1.6 fusion.1
  233.3 1.6 fusion.2
  234.9 1.6 fusion.3
  236.5 0.1 pad_maximum_fusion
  236.5 1.3 copy.41
  237.8 0.0 copy-done.2
  (8 shorter events, 0.1 us)
Async XLA Ops:
  7.2 11.2 %copy-start = (bf16[256,512]{1,0:T(8,128)(2,1)S(1)}, bf16[256,512]{1,0:T(8,128)(2,1)}, u32[]{:S(2)}) copy-start(bf16[256,512]{1,0:T(8,128)(2,1)} %param.13) | copy-start | bytes 786436
  7.2 37.8 %all-gather.4.cloned.1.call-start = ((), (), s32[]{:S(2)}) async-start(), calls=%async_computation | async-start | bytes 1638400 | tf_op jit(solution)/shard_map/all_gather | solution.py:45
  7.9 126.5 %all-gather.6.cloned.1.call-start = ((), (), s32[]{:S(2)}) async-start(), calls=%async_computation.2 | async-start | bytes 11796480 | tf_op jit(solution)/shard_map/all_gather | solution.py:53
  54.6 9.2 %copy-start.3 = (f32[512,64]{0,1:T(8,128)S(1)}, f32[512,64]{0,1:T(8,128)}, u32[]{:S(2)}) copy-start(f32[512,64]{0,1:T(8,128)} %param.15) | copy-start | bytes 393220
  59.9 4.0 %copy-start.1 = (f32[5120,512]{0,1:T(8,128)}, f32[5120,512]{0,1:T(8,128)S(1)}, u32[]{:S(2)}) copy-start(f32[5120,512]{0,1:T(8,128)S(1)} %fusion.9) | copy-start | bytes 31457284
  72.0 157.2 %all-reduce.2.cloned.1.call-start = ((), (), s32[]{:S(2)}) async-start(), calls=%async_computation.1 | async-start | bytes 262144 | tf_op jit(solution)/shard_map/psum | solution.py:58
  230.1 7.8 %copy-start.2 = (f32[512,64]{0,1:T(8,128)}, f32[512,64]{0,1:T(8,128)S(1)}, u32[]{:S(2)}) copy-start(f32[512,64]{0,1:T(8,128)S(1)} %broadcast_multiply_fusion) | copy-start | bytes 393220
Sparse Core Ops, SparseCore 0:
  9.6 35.3 all-gather.3
  72.1 62.2 all-gather.5
  176.2 52.9 all-reduce.1
